TPU v7x, 128 devices: a whole 4x4x4 slice. The times are simulated.
128 devices in a mesh: row: 16 (over x, z), col: 8 (over y, core).
Axes of the slice: x: 4, y: 4, z: 4, core: 2. Of those that a mesh axis runs over, the one named last changes fastest.
Arguments:
- front: float32 [6, 2048, 12, 1024], P(None, 'row', None, 'col')
- children: float32 [32768, 8192], P('row', 'col')
- block_map: int32 [4, 64], replicated, may hold values from -1 to 95, as said below
- child_at: int32 [4], replicated, may hold values from 0 to 3, each once
Outputs:
- factored: float32 [6, 2048, 12, 1024], P(None, 'row', None, 'col')
Inputs may be any that keep to these rules, and one draw needn't show every extreme that they name: Entry block_map[k, t * 16 + p] is -1 or a parent block b with b % 16 == p. For each child k and each p the entries that are not -1 come first in t, increase, and number 4 // 2 to 4; for every child both of these counts occur. No block appears twice for one child. `child_at`: each child stands in exactly one slot.
All inputs are finite; a program needn't handle non-finite values.
Results may differ from a plain program's by a relative error of at most 0.00005.
Values sent between devices are 32-bit elements; how exact they have to be, the bound alone decides.
A program may use at most 192 MiB of HBM per device.

v0:
```python
import jax
import jax.numpy as jnp
from jax import lax
from jax.sharding import PartitionSpec as P

CHILD = 4
PB = 8


HIGHEST_PRECISION = lax.Precision.HIGHEST


def from_root(value, axis, root):
    mine = lax.axis_index(axis) == root
    return lax.psum(jnp.where(mine, value, jnp.zeros_like(value)), axis)


def widen_columns(local_rows, col_onehot, row_index, per_device, slot_cap):
    owners = (row_index * per_device + jnp.arange(per_device)) // slot_cap
    chosen = jnp.take(col_onehot, owners, axis=0)
    return jnp.einsum("lpxsy,lsb->lpxby", local_rows, chosen, precision=HIGHEST_PRECISION)


def body(front, children, block_map, child_at):
    grid_rows = lax.axis_size("row")
    grid_cols = lax.axis_size("col")
    row_index = lax.axis_index("row")
    col_index = lax.axis_index("col")
    tile_rows = front.shape[0]
    block_size = front.shape[1]
    tile_cols = front.shape[2]
    slot_cap = block_map.shape[1] // grid_rows
    fanout = grid_rows // grid_cols
    group_cap = slot_cap * fanout
    per_device = CHILD * slot_cap // grid_rows
    panel_width = PB * block_size
    panel_tiles = (PB + grid_cols - 1) // grid_cols
    diag_tiles = (PB + grid_rows - 1) // grid_rows
    slot_maps = jnp.take(block_map, child_at, axis=0)
    own_maps = jnp.take(slot_maps.reshape(CHILD, slot_cap, grid_rows), row_index, axis=2)
    row_onehot = (
        (own_maps[:, :, None] >= 0)
        & (own_maps[:, :, None] // grid_rows == jnp.arange(tile_rows)[None, None, :])
    ).astype(jnp.float32)
    columns = jnp.take(slot_maps.reshape(CHILD, slot_cap, fanout, grid_cols), col_index, axis=3)
    columns = columns.transpose(0, 2, 1).reshape(CHILD, group_cap)
    col_onehot = (
        (columns[:, :, None] >= 0)
        & (columns[:, :, None] // grid_cols == jnp.arange(tile_cols)[None, None, :])
    ).astype(jnp.float32)
    local_rows = children.reshape(per_device, grid_rows, block_size, group_cap, block_size)
    assembled = None
    widened = widen_columns(local_rows, col_onehot, row_index, per_device, slot_cap)
    received = lax.all_to_all(widened, "row", split_axis=1, concat_axis=0, tiled=True)
    shaped = received.reshape(CHILD, slot_cap, received.shape[2], received.shape[3], block_size)
    assembled = front + jnp.einsum(
        "cta,ctxby->axby", row_onehot, shaped, precision=HIGHEST_PRECISION
    )
    panel_part = assembled[:, :, :panel_tiles]
    gathered = lax.all_gather(
        panel_part.reshape(tile_rows * block_size, panel_tiles, 1, block_size),
        "col",
        axis=2,
        tiled=True,
    )
    panel_rows = gathered.reshape(tile_rows * block_size, panel_tiles * grid_cols * block_size)
    picked = panel_rows.reshape(tile_rows, block_size, panel_width)[:diag_tiles][:, None]
    stacked = lax.all_gather(picked, "row", axis=1, tiled=True)
    corner = stacked.reshape(diag_tiles * grid_rows * block_size, panel_width)[:panel_width]
    factor = jnp.linalg.cholesky(0.5 * (corner + corner.T))
    solved = jax.scipy.linalg.solve_triangular(factor, panel_rows.T, lower=True).T
    global_rows = (
        jnp.arange(tile_rows)[:, None] * grid_rows + row_index
    ) * block_size + jnp.arange(block_size)[None, :]
    flat_rows = global_rows.reshape(-1)
    top_rows = jnp.take(factor, jnp.clip(flat_rows, 0, panel_width - 1), axis=0)
    panel_out = jnp.where((flat_rows < panel_width)[:, None], top_rows, solved)
    pieces = []
    for offset in range(fanout):
        pieces.append(
            from_root(
                solved.reshape(tile_rows, block_size, panel_width),
                "row",
                col_index + offset * grid_cols,
            )
        )
    across = jnp.stack(pieces, axis=1).reshape(tile_cols * block_size, panel_width)
    product = jnp.dot(solved, across.T, precision=HIGHEST_PRECISION).reshape(
        tile_rows, block_size, tile_cols, block_size
    )
    global_cols = (
        jnp.arange(tile_cols)[:, None] * grid_cols + col_index
    ) * block_size + jnp.arange(block_size)[None, :]
    inside = (global_rows >= panel_width)[:, :, None, None] & (global_cols >= panel_width)[
        None, None, :, :
    ]
    updated = jnp.where(inside, assembled - product, assembled)
    head_cols = global_cols[:panel_tiles].reshape(-1)
    head_part = jnp.take(panel_out, jnp.clip(head_cols, 0, panel_width - 1), axis=1).reshape(
        tile_rows, block_size, panel_tiles, block_size
    )
    head_part = jnp.where(
        (global_cols[:panel_tiles] < panel_width)[None, None],
        head_part,
        updated[:, :, :panel_tiles],
    )
    return jnp.concatenate([head_part, updated[:, :, panel_tiles:]], axis=2)


def solution(mesh):
    in_specs = (P(None, "row", None, "col"), P("row", "col"), P(), P())
    out_specs = P(None, "row", None, "col")
    return jax.shard_map(body, mesh=mesh, in_specs=in_specs, out_specs=out_specs, check_vma=False)
```

profile of v0, /device:TPU:1, one launch (start us, length us, event | category | flops | bytes accessed | tf_op | source)
XLA Modules:
  0.0 966.9 jit_solution(6749736399424785142)
XLA Ops:
  9.0 5.5 copy.81
  14.5 16.7 %convolution_bitcast_fusion = f32[1,16,128,12,128]{4,3,2,1,0:T(8,128)} fusion(s32[1,8]{1,0:T(1,128)S(1)} %constant_dynamic-slice_fusion.4, pred[1,8]{1,0:T(4,128)(4,1)S(1)} %constant_dynamic-slice_fusion.1, pred[]{:T(512)} %bitcast.8, f32[16,128,8,128]{3,2,1,0:T(8,128)S(1)} %bitcast.214), kind=kOutput, calls=%fused_computation.6 | convolution fusion | flops 301990272 | bytes 20971560 | tf_op jit(solution)/shard_map/lpxsy,lsb->lpxby/dot_general | solution.py:21
  31.2 14.2 %copy.55 = f32[1,16,128,12,128]{4,2,3,0,1:T(8,128)} copy(f32[1,16,128,12,128]{4,3,2,1,0:T(8,128)} %convolution_bitcast_fusion) | data formatting | bytes 25165824 | tf_op jit(solution)/shard_map/lpxsy,lsb->lpxby/transpose | solution.py:21
  45.4 8.5 all-to-all-start
  54.6 216.0 %all-to-all-done = f32[1,16,128,12,128]{4,2,3,0,1:T(8,128)} async-done(((f32[1,16,128,12,128]{4,2,3,0,1:T(8,128)}), f32[1,16,128,12,128]{4,2,3,0,1:T(8,128)}, u32[]{:S(2)}, u32[]{:S(2)}) %all-to-all-start) | async-done | bytes 12582944 | tf_op jit(solution)/shard_map/all_to_all | solution.py:54
  270.6 16.3 %copy.56 = f32[1,16,128,12,128]{4,1,3,2,0:T(8,128)} copy(f32[1,16,128,12,128]{4,2,3,0,1:T(8,128)} %all-to-all-done) | data formatting | bytes 25165824 | tf_op jit(solution)/shard_map/all_to_all | solution.py:54
  286.9 14.9 %bitcast_add_fusion = f32[6,128,12,128]{3,0,2,1:T(8,128)S(1)} fusion(f32[6,128,12,128]{3,1,2,0:T(8,128)} %param.4, f32[4,4,128,12,128]{4,1,0,3,2:T(4,128)} %bitcast.215, s32[4,4]{1,0:T(4,128)S(1)} %add_select_fusion.1, pred[4,4]{1,0:T(4,128)(4,1)S(1)} %bitcast_compare_fusion.1), kind=kOutput, calls=%fused_computation.10 | convolution fusion | flops 227672256 | bytes 22020176 | tf_op jit(solution)/shard_map/cta,ctxby->axby/dot_general | solution.py:56
  305.5 36.8 %all-gather.3.cloned.1.call-done = f32[768,1,8,128]{3,0,1,2:T(8,128)} async-done(((f32[768,1,1,128]{3,0,1,2:T(8,128)}), f32[768,1,8,128]{3,0,1,2:T(8,128)}) %all-gather.3.cloned.1.call-update) | async-done | bytes 3145744 | tf_op jit(solution)/shard_map/all_gather | solution.py:60
  348.1 70.4 %all-gather.5.cloned.1.call-done = f32[1,16,128,1024]{3,2,0,1:T(8,128)} async-done(((f32[1,1,128,1024]{3,2,0,1:T(8,128)}), f32[1,16,128,1024]{3,2,0,1:T(8,128)}) %all-gather.5.cloned.1.call-update) | async-done | bytes 8388624 | tf_op jit(solution)/shard_map/all_gather | solution.py:68
  418.4 4.8 slice.325
  423.2 5.3 copy.78
  428.6 6.8 fusion.2
  435.4 13.8 %copy.64 = f32[1024,1024]{0,1:T(8,128)} copy(f32[1024,1024]{1,0:T(8,128)} %fusion.2) | data formatting | bytes 8388608 | tf_op jit(solution)/shard_map/mul | solution.py:70
  449.2 4.4 fusion.1
  455.6 11.7 %cholesky.223 = f32[128,128]{1,0:T(8,128)S(1)} custom-call(f32[128,128]{1,0:T(8,128)S(1)} %cholesky.580), custom_call_target="Cholesky" | custom-call | tf_op jit(solution)/shard_map/jit(cholesky)/cholesky | solution.py:70
  467.4 9.8 %custom-call.63 = f32[1,128,128]{1,2,0:T(8,128)S(1)} custom-call(f32[1,128,128]{2,1,0:T(8,128)S(1)} %get-tuple-element.108), custom_call_target="InvertDiagBlocksLowerTriangular" | custom-call | tf_op jit(solution)/shard_map/jit(cholesky)/cholesky | solution.py:70
  483.6 11.9 %cholesky.244 = f32[128,128]{1,0:T(8,128)S(1)} custom-call(f32[128,128]{1,0:T(8,128)S(1)} %cholesky.584), custom_call_target="Cholesky" | custom-call | tf_op jit(solution)/shard_map/jit(cholesky)/cholesky | solution.py:70
  496.1 9.8 %custom-call.64 = f32[1,128,128]{1,2,0:T(8,128)S(1)} custom-call(f32[1,128,128]{2,1,0:T(8,128)S(1)} %get-tuple-element.105), custom_call_target="InvertDiagBlocksLowerTriangular" | custom-call | tf_op jit(solution)/shard_map/jit(cholesky)/cholesky | solution.py:70
  509.3 11.7 %cholesky.468 = f32[128,128]{1,0:T(8,128)S(1)} custom-call(f32[128,128]{1,0:T(8,128)S(1)} %cholesky.589), custom_call_target="Cholesky" | custom-call | tf_op jit(solution)/shard_map/jit(cholesky)/cholesky | solution.py:70
  522.3 9.8 %custom-call.65 = f32[1,128,128]{1,2,0:T(8,128)S(1)} custom-call(f32[1,128,128]{2,1,0:T(8,128)S(1)} %get-tuple-element.102), custom_call_target="InvertDiagBlocksLowerTriangular" | custom-call | tf_op jit(solution)/shard_map/jit(cholesky)/cholesky | solution.py:70
  535.6 12.1 %cholesky.487 = f32[128,128]{1,0:T(8,128)S(1)} custom-call(f32[128,128]{1,0:T(8,128)S(1)} %cholesky.594), custom_call_target="Cholesky" | custom-call | tf_op jit(solution)/shard_map/jit(cholesky)/cholesky | solution.py:70
  549.0 9.8 %custom-call.66 = f32[1,128,128]{1,2,0:T(8,128)S(1)} custom-call(f32[1,128,128]{2,1,0:T(8,128)S(1)} %get-tuple-element.99), custom_call_target="InvertDiagBlocksLowerTriangular" | custom-call | tf_op jit(solution)/shard_map/jit(cholesky)/cholesky | solution.py:70
  562.3 11.7 %cholesky.506 = f32[128,128]{1,0:T(8,128)S(1)} custom-call(f32[128,128]{1,0:T(8,128)S(1)} %cholesky.599), custom_call_target="Cholesky" | custom-call | tf_op jit(solution)/shard_map/jit(cholesky)/cholesky | solution.py:70
  575.3 9.9 %custom-call.67 = f32[1,128,128]{1,2,0:T(8,128)S(1)} custom-call(f32[1,128,128]{2,1,0:T(8,128)S(1)} %get-tuple-element.96), custom_call_target="InvertDiagBlocksLowerTriangular" | custom-call | tf_op jit(solution)/shard_map/jit(cholesky)/cholesky | solution.py:70
  588.6 11.7 %cholesky.526 = f32[128,128]{1,0:T(8,128)S(1)} custom-call(f32[128,128]{1,0:T(8,128)S(1)} %cholesky.604), custom_call_target="Cholesky" | custom-call | tf_op jit(solution)/shard_map/jit(cholesky)/cholesky | solution.py:70
  601.6 9.8 %custom-call.68 = f32[1,128,128]{1,2,0:T(8,128)S(1)} custom-call(f32[1,128,128]{2,1,0:T(8,128)S(1)} %get-tuple-element.93), custom_call_target="InvertDiagBlocksLowerTriangular" | custom-call | tf_op jit(solution)/shard_map/jit(cholesky)/cholesky | solution.py:70
  614.4 12.0 %cholesky.546 = f32[128,128]{1,0:T(8,128)S(1)} custom-call(f32[128,128]{1,0:T(8,128)S(1)} %cholesky.609), custom_call_target="Cholesky" | custom-call | tf_op jit(solution)/shard_map/jit(cholesky)/cholesky | solution.py:70
  627.7 9.8 %custom-call.69 = f32[1,128,128]{1,2,0:T(8,128)S(1)} custom-call(f32[1,128,128]{2,1,0:T(8,128)S(1)} %get-tuple-element.90), custom_call_target="InvertDiagBlocksLowerTriangular" | custom-call | tf_op jit(solution)/shard_map/jit(cholesky)/cholesky | solution.py:70
  640.1 11.7 %cholesky.564 = f32[128,128]{1,0:T(8,128)S(1)} custom-call(f32[128,128]{1,0:T(8,128)S(1)} %convolution_subtract_fusion.12), custom_call_target="Cholesky" | custom-call | tf_op jit(solution)/shard_map/jit(cholesky)/cholesky | solution.py:70
  658.8 6.8 fusion.3
  665.6 27.6 %while.4 = (s32[]{:T(128)}, f32[1024,1024]{1,0:T(8,128)}, s32[8,2]{0,1:T(2,128)S(1)}, f32[8,128,128]{2,1,0:T(8,128)}, s32[]{:T(128)}) while((s32[]{:T(128)}, f32[1024,1024]{1,0:T(8,128)}, s32[8,2]{0,1:T(2,128)S(1)}, f32[8,128,128]{2,1,0:T(8,128)}, s32[]{:T(128)}) %tuple.76), condition=%wide.while_cond.3, body=%wide.while_body.3.sunk | while | flops 2 | bytes 132205 | solution.py:71
  666.2 2.8 bitcast_dynamic-update-slice_fusion.2
  669.7 2.8 bitcast_dynamic-update-slice_fusion.2
  673.1 2.8 bitcast_dynamic-update-slice_fusion.2
  676.6 2.8 bitcast_dynamic-update-slice_fusion.2
  683.5 2.8 bitcast_dynamic-update-slice_fusion.2
  687.0 2.8 bitcast_dynamic-update-slice_fusion.2
  693.2 80.2 %custom-call.70 = f32[8,128,128]{1,2,0:T(8,128)} custom-call(f32[8,128,128]{2,1,0:T(8,128)} %get-tuple-element.36), custom_call_target="InvertDiagBlocksLowerTriangular" | custom-call | tf_op jit(solution)/shard_map/jit(_solve_triangular)/triangular_solve | solution.py:71
  796.8 5.6 select_bitcast_fusion.1
  803.1 6.8 gather_fusion.1
  810.0 4.4 copy.65
  814.4 4.1 select_select_fusion.1
  818.5 3.0 gather_fusion.2
  821.7 103.0 %all-reduce.4.cloned.1.call-done = (f32[6,1,128,1024]{3,2,0,1:T(8,128)}, f32[6,1,128,1024]{3,2,0,1:T(8,128)}) async-done(((f32[6,1,128,1024]{3,2,0,1:T(8,128)}, f32[6,1,128,1024]{3,2,0,1:T(8,128)}), (f32[6,1,128,1024]{3,2,0,1:T(8,128)}, f32[6,1,128,1024]{3,2,0,1:T(8,128)})) %all-reduce.4.cloned.1.call-update) | async-done | bytes 6291472 | tf_op jit(solution)/shard_map/psum | solution.py:15
  924.6 3.4 pad_maximum_fusion
  929.9 16.0 %fusion.99 = f32[6,128,12,128]{3,1,2,0:T(8,128)S(1)} fusion(f32[6,128,1024,1]{2,1,3,0:T(8,128)S(1)} %bitcast.229, f32[12,128,1024,1]{2,1,0,3:T(8,128)S(1)} %bitcast.231), kind=kOutput, calls=%fused_computation.239 | convolution fusion | flops 14495514624 | bytes 14155776 | tf_op jit(solution)/shard_map/dot_general | solution.py:88
  945.9 7.5 subtract_select_fusion
  955.0 4.9 copy.73
  (143 shorter events, 87.3 us)
Async XLA Ops:
  6.5 1.3 copy-start
  45.4 225.2 %all-to-all-start = ((f32[1,16,128,12,128]{4,2,3,0,1:T(8,128)}), f32[1,16,128,12,128]{4,2,3,0,1:T(8,128)}, u32[]{:S(2)}, u32[]{:S(2)}) async-start(f32[1,16,128,12,128]{4,2,3,0,1:T(8,128)} %copy.55), calls=%async_computation | async-start | bytes 25165824 | tf_op jit(solution)/shard_map/all_to_all | solution.py:54
  53.9 288.4 %all-gather.3.cloned.1.call-start = ((), (), s32[]{:S(2)}) async-start(), calls=%async_computation.1 | async-start | bytes 3538944 | tf_op jit(solution)/shard_map/all_gather | solution.py:60
  301.8 2.7 copy-start.2
  305.5 113.0 %all-gather.5.cloned.1.call-start = ((), (), s32[]{:S(2)}) async-start(), calls=%async_computation.2 | async-start | bytes 8912896 | tf_op jit(solution)/shard_map/all_gather | solution.py:68
  344.7 78.6 %copy-start.3 = (f32[768,1,8,128]{0,3,2,1:T(8,128)}, f32[768,1,8,128]{0,3,2,1:T(8,128)S(1)}, u32[]{:S(2)}) copy-start(f32[768,1,8,128]{0,3,2,1:T(8,128)S(1)} %copy.60) | copy-start | bytes 9437188
  348.0 576.6 %all-reduce.4.cloned.1.call-start = ((), (), s32[]{:S(2)}) async-start(), calls=%async_computation.3 | async-start | bytes 12582912 | tf_op jit(solution)/shard_map/psum | solution.py:15
  453.7 1.9 copy-start.6
  773.4 6.5 copy-start.7
  775.1 5.4 copy-start.4
  928.0 1.9 copy-start.5
  928.0 17.8 %slice-start = ((s8[6291456]{0:T(1024)(128)(4,1)}), s8[2097152]{0:T(1024)(128)(4,1)S(1)}, s32[]{:S(2)}) async-start(s8[6291456]{0:T(1024)(128)(4,1)} %bitcast.217), calls=%async_computation.4 | async-start | bytes 4194304
  929.9 16.0 %slice-start.1 = ((s8[6291456]{0:T(1024)(128)(4,1)}), s8[4194304]{0:T(1024)(128)(4,1)S(1)}, s32[]{:S(2)}) async-start(s8[6291456]{0:T(1024)(128)(4,1)} %bitcast.217), calls=%async_computation.5 | async-start | bytes 8388608
  954.1 5.8 copy-start.1
Sparse Core Ops, SparseCore 0:
  305.6 36.6 all-gather.2
  348.1 70.2 all-gather.4
  802.6 121.9 all-reduce.3
where the time goes:
time: 976 us; the launch traced here: 967 us
  waiting for transfers between devices  426 us (44%)
  other arithmetic  295 us (30%)
  local copies, waits for them, and re-layouts  127 us (13%)
  matrix products  91.4 us (9%)
  between operations  19.1 us (2%)
    all_to_all x1, waiting for transfers between devices, body(): lax.all_to_all(widened, 'row', split_axis=1, concat_axis=0, tiled=True)  216 us
    another operation x30, other arithmetic, body(): factor = jnp.linalg.cholesky(0.5 * (corner + corner.T))  173 us
    psum x1, waiting for transfers between devices, from_root(): return lax.psum(jnp.where(mine, value, jnp.zeros_like(value)), axis)  103 us
    another operation x3, other arithmetic, body(): jax.scipy.linalg.solve_triangular(factor, panel_rows.T, lower=True)  87 us
    all_gather x1, waiting for transfers between devices, body(): stacked = lax.all_gather(picked, 'row', axis=1, tiled=True)  70.4 us
    all_gather x1, waiting for transfers between devices, body(): lax.all_gather(panel_part.reshape(tile_rows * block_size, panel_tiles, 1,...  36.8 us
    another operation x24, local copies, waits for them, and re-layouts  27.6 us
    another operation x14, matrix products, body(): factor = jnp.linalg.cholesky(0.5 * (corner + corner.T))  23 us
  transfers between devices with their start and end apart: 4, of which 4 were waited for; matrix products, arithmetic and copies ran while one was open for 2% of the time, Pallas kernels for 0%

commit v1 on v0

v1 whole, which is shorter than its diff:
```python
import functools
import jax
import jax.numpy as jnp
from jax import lax
from jax.experimental import pallas as pl
from jax.experimental.pallas import tpu as pltpu
from jax.sharding import PartitionSpec as P

F32 = jnp.float32
BF16 = jnp.bfloat16
HIGHEST = lax.Precision.HIGHEST
CHILD = 4
BS = 128
NT = ((1,), (1,))
NN = ((1,), (0,))
VMEM_SPEC = pl.BlockSpec(memory_space=pltpu.VMEM)
SMEM_SPEC = pl.BlockSpec(memory_space=pltpu.SMEM)


def mm(a, b, dims):
    return lax.dot_general(a, b, (dims, ((), ())), precision=HIGHEST, preferred_element_type=F32)


def split(x):
    hi = x.astype(BF16)
    return hi, (x - hi.astype(F32)).astype(BF16)


def mm3(a, b, dims):
    dot = functools.partial(
        lax.dot_general, dimension_numbers=(dims, ((), ())), preferred_element_type=F32
    )
    return dot(a[0], b[0]) + (dot(a[0], b[1]) + dot(a[1], b[0]))


def diag_factor(get, put_u, put_x):
    sub = lax.broadcasted_iota(jnp.int32, (8, 128), 0)
    lane = lax.broadcasted_iota(jnp.int32, (8, 128), 1)
    d = [get(i) for i in range(16)]
    x = [(lane == sub + 8 * i).astype(F32) for i in range(16)]

    def panel(i, carry):
        d, x = list(carry[0]), list(carry[1])
        for j in range(8):
            c0 = jnp.broadcast_to(d[0][:, j:j + 1], (8, 128))
            r = lax.rsqrt(jnp.broadcast_to(c0[j:j + 1, :], (8, 128)))
            ud = jnp.broadcast_to(d[0][j:j + 1, :], (8, 128)) * r
            ux = jnp.broadcast_to(x[0][j:j + 1, :], (8, 128)) * r
            m = jnp.where(sub > j, c0 * r, 0.0)
            d[0] = jnp.where(sub == j, ud, d[0] - m * ud)
            x[0] = jnp.where(sub == j, ux, x[0] - m * ux)
            for k in range(1, 16):
                m = jnp.broadcast_to(d[k][:, j:j + 1], (8, 128)) * r
                d[k] = d[k] - m * ud
                x[k] = x[k] - m * ux
        row = d[0]
        row = pltpu.roll(row, 8 * i, 1)
        put_u(i, jnp.where(lane >= sub + 8 * i, row, 0.0))
        put_x(i, x[0])
        nd = [pltpu.roll(v, 120, 1) for v in d[1:]] + [jnp.zeros((8, 128), F32)]
        nx = x[1:] + [jnp.zeros((8, 128), F32)]
        return tuple(nd), tuple(nx)

    lax.fori_loop(0, 16, panel, (tuple(d), tuple(x)))


def chol_kernel(n, c_ref, l_ref, m_ref, u_ref, x_ref):
    def blk(i, j):
        return (pl.ds(i * BS, BS), pl.ds(j * BS, BS))

    def corner(i, j):
        return jnp.concatenate([c_ref[i * n + j], c_ref[(i + n) * n + j]], axis=0)

    for i in range(n):
        for j in range(i + 1):
            l_ref[blk(i, j)] = 0.5 * (corner(i, j) + corner(j, i).T)
        for j in range(i + 1, n):
            l_ref[blk(i, j)] = jnp.zeros((BS, BS), F32)

    def put_u(i, v):
        u_ref[pl.ds(pl.multiple_of(8 * i, 8), 8), :] = v

    def put_x(i, v):
        x_ref[pl.ds(pl.multiple_of(8 * i, 8), 8), :] = v

    for k in range(n):
        diag_factor(lambda i, k=k: l_ref[pl.ds(k * BS + 8 * i, 8), pl.ds(k * BS, BS)], put_u, put_x)
        l_ref[blk(k, k)] = u_ref[...].T
        x = x_ref[...]
        h = k % 2
        m_ref[k // 2, h * BS : (h + 1) * BS, h * BS : (h + 1) * BS] = x
        if h == 1:
            m_ref[k // 2, 0:BS, BS : 2 * BS] = jnp.zeros((BS, BS), F32)
            t = mm(l_ref[blk(k, k - 1)], m_ref[k // 2, 0:BS, 0:BS], NN)
            m_ref[k // 2, BS : 2 * BS, 0:BS] = -mm(x, t, NN)
        if k + 1 < n:
            lo = (k + 1) * BS
            rest = n * BS - lo
            col = mm(l_ref[pl.ds(lo, rest), pl.ds(k * BS, BS)], x, NT)
            l_ref[pl.ds(lo, rest), pl.ds(k * BS, BS)] = col
            for j in range(k + 1, n):
                o = (j - k - 1) * BS
                l_ref[pl.ds(j * BS, n * BS - j * BS), pl.ds(j * BS, BS)] -= mm(
                    col[o:], col[o : o + BS], NT
                )


def cholesky(corner):
    n = 8
    return pl.pallas_call(
        functools.partial(chol_kernel, n),
        out_shape=(
            jax.ShapeDtypeStruct((n * BS, n * BS), F32),
            jax.ShapeDtypeStruct((n // 2, 2 * BS, 2 * BS), F32),
        ),
        in_specs=[VMEM_SPEC],
        out_specs=(VMEM_SPEC, VMEM_SPEC),
        scratch_shapes=[pltpu.VMEM((BS, BS), F32), pltpu.VMEM((BS, BS), F32)],
        cost_estimate=pl.CostEstimate(
            flops=100_000_000_000, bytes_accessed=9_000_000, transcendentals=0
        ),
        name="cholesky",
    )(corner)


def assemble_kernel(bm_ref, at_ref, front_ref, recv_ref, out_ref):
    p = lax.axis_index("row")
    q = lax.axis_index("col")
    out_ref[...] = front_ref[:, 0]
    for c in range(CHILD):
        k = at_ref[c]
        hit = bm_ref[k, q] == q
        for t in range(4):
            r = bm_ref[k, t * 16 + p]

            @pl.when(jnp.logical_and(hit, r >= 0))
            def _(r=r, s=c * 4 + t):
                out_ref[r >> 4] += recv_ref[s]


def assemble_panel(block_map, child_at, front, recv):
    return pl.pallas_call(
        assemble_kernel,
        grid=(1,),
        out_shape=jax.ShapeDtypeStruct((6, BS, BS), F32),
        in_specs=[
            SMEM_SPEC,
            SMEM_SPEC,
            pl.BlockSpec((6, 1, BS, BS), lambda i: (0, 0, 0, 0)),
            pl.BlockSpec((16, BS, BS), lambda i: (0, 0, 0)),
        ],
        out_specs=pl.BlockSpec((6, BS, BS), lambda i: (0, 0, 0)),
        name="assemble_panel",
    )(block_map, child_at, front, recv)


def update_kernel(
    bm_ref, at_ref, front_ref, recv0_ref, recv1_ref, rrow_ref, rcol_ref, l_ref, m_ref, out_ref,
    lh_ref, ll_ref, mh_ref, ml_ref, yf_ref, yh_ref, yl_ref, zh_ref, zl_ref,
):
    step = pl.program_id(0)
    p = lax.axis_index("row")
    q = lax.axis_index("col")
    W = 2 * BS

    def solve(rhs, rows, yh, yl, yf):
        for k in range(4):
            t = rhs(k)
            for j in range(k):
                js = pl.ds(j * W, W)
                ks = pl.ds(k * W, W)
                t = t - mm3((yh[:, js], yl[:, js]), (lh_ref[ks, js], ll_ref[ks, js]), NT)
            y = mm3(split(t), (mh_ref[k], ml_ref[k]), NT)
            ks = pl.ds(k * W, W)
            if yf is not None:
                yf[:, ks] = y
            yh[:, ks], yl[:, ks] = split(y)

    @pl.when(step == 0)
    def _():
        for k in range(4):
            mh_ref[k], ml_ref[k] = split(m_ref[k])
            for j in range(k):
                js = pl.ds(j * W, W)
                ks = pl.ds(k * W, W)
                lh_ref[ks, js], ll_ref[ks, js] = split(l_ref[ks, js])
        solve(
            lambda k: jnp.concatenate([rrow_ref[2 * k], rrow_ref[2 * k + 1]], axis=1),
            768, yh_ref, yl_ref, yf_ref,
        )

    def rcol(k):
        return jnp.concatenate(
            [
                jnp.concatenate([rcol_ref[8 * e + 2 * k], rcol_ref[8 * e + 2 * k + 1]], axis=1)
                for e in range(2)
            ],
            axis=0,
        )

    solve(rcol, 256, zh_ref, zl_ref, None)
    prod = mm3((yh_ref[...], yl_ref[...]), (zh_ref[...], zl_ref[...]), NT)
    for a in range(6):
        for e in range(2):
            part = prod[a * BS : (a + 1) * BS, e * BS : (e + 1) * BS]
            if a == 0:
                part = jnp.where(p < 8, 0.0, part)
            out_ref[a, e] = front_ref[a, e] - part

    for c in range(CHILD):
        k = at_ref[c]
        for s2 in range(8):
            h = bm_ref[k, (s2 % 4) * 16 + (s2 // 4) * 8 + q]
            b = h >> 3

            @pl.when(jnp.logical_and(h >= 0, (b >> 1) == step))
            def _(c=c, s2=s2, b=b, k=k):
                for t in range(4):
                    r = bm_ref[k, t * 16 + p]

                    @pl.when(r >= 0)
                    def _(r=r, s=c * 4 + t):
                        if s2 == 0:
                            blk = recv0_ref[s]
                        else:
                            blk = recv1_ref[s, :, (s2 - 1) * BS : s2 * BS]
                        out_ref[r >> 4, b & 1] += blk

    @pl.when(step == 0)
    def _():
        cs = pl.ds(pl.multiple_of(q * BS, BS), BS)
        for a in range(6):
            out_ref[a, 0] = yf_ref[a * BS : (a + 1) * BS, cs]

        @pl.when(p < 8)
        def _():
            out_ref[0, 0] = l_ref[pl.ds(pl.multiple_of(jnp.minimum(p, 7) * BS, BS), BS), cs]


def update(block_map, child_at, front, recv0, recv1, rrow, rcol, l, m):
    one = pl.Buffered(1)
    return pl.pallas_call(
        update_kernel,
        grid=(6,),
        out_shape=jax.ShapeDtypeStruct((6, 12, BS, BS), F32),
        in_specs=[
            SMEM_SPEC,
            SMEM_SPEC,
            pl.BlockSpec((6, 2, BS, BS), lambda i: (0, i, 0, 0)),
            pl.BlockSpec((16, BS, BS), lambda i: (0, 0, 0), pipeline_mode=one),
            pl.BlockSpec((16, BS, 7 * BS), lambda i: (0, 0, 0), pipeline_mode=one),
            pl.BlockSpec((8, 768, BS), lambda i: (0, 0, 0), pipeline_mode=one),
            pl.BlockSpec((16, BS, BS), lambda i: (0, i, 0)),
            pl.BlockSpec((1024, 1024), lambda i: (0, 0), pipeline_mode=one),
            pl.BlockSpec((4, 2 * BS, 2 * BS), lambda i: (0, 0, 0), pipeline_mode=one),
        ],
        out_specs=pl.BlockSpec((6, 2, BS, BS), lambda i: (0, i, 0, 0)),
        scratch_shapes=[
            pltpu.VMEM((1024, 1024), BF16),
            pltpu.VMEM((1024, 1024), BF16),
            pltpu.VMEM((4, 2 * BS, 2 * BS), BF16),
            pltpu.VMEM((4, 2 * BS, 2 * BS), BF16),
            pltpu.VMEM((768, 1024), F32),
            pltpu.VMEM((768, 1024), BF16),
            pltpu.VMEM((768, 1024), BF16),
            pltpu.VMEM((256, 1024), BF16),
            pltpu.VMEM((256, 1024), BF16),
        ],
        compiler_params=pltpu.CompilerParams(vmem_limit_bytes=60 * 1024 * 1024),
        cost_estimate=pl.CostEstimate(
            flops=18_000_000_000, bytes_accessed=36_000_000, transcendentals=0
        ),
        name="update",
    )(block_map, child_at, front, recv0, recv1, rrow, rcol, l, m)


def body(front, children, block_map, child_at):
    p = lax.axis_index("row")
    front4 = front.transpose(0, 2, 1, 3)
    slots = children.reshape(16, BS, 8 * BS)
    recv0 = lax.all_to_all(slots[:, :, :BS], "row", 0, 0)
    panel = assemble_panel(block_map, child_at, front4, recv0)
    low = lax.ppermute(panel[0, 64:], "row", [(i, i + 8) for i in range(8)])
    piece = jnp.where(p < 8, panel[0, :64], low)
    corner = lax.all_gather(piece, ("row", "col"))
    corner, panel, rest = lax.optimization_barrier((corner, panel, slots[:, :, BS:]))
    flat = panel.reshape(768, BS)
    moved = lax.ppermute(
        flat,
        ("row", "col"),
        [
            (r * 8 + c, ((r // 8) * 8 + c) * 8 + r % 8)
            for r in range(16)
            for c in range(8)
        ],
    )
    rcol = lax.all_gather(moved, "row")
    rrow = lax.all_gather(flat, "col")
    recv1 = lax.all_to_all(rest, "row", 0, 0)
    l, m = cholesky(corner)
    out = update(block_map, child_at, front4, recv0, recv1, rrow, rcol, l, m)
    return out.transpose(0, 2, 1, 3)


def solution(mesh):
    in_specs = (P(None, "row", None, "col"), P("row", "col"), P(), P())
    out_specs = P(None, "row", None, "col")
    return jax.shard_map(body, mesh=mesh, in_specs=in_specs, out_specs=out_specs, check_vma=False)
```

time: 976 us -> 336 us (0.34)
  waiting for transfers between devices: 426 us -> 81.2 us
  other arithmetic: 295 us -> 1.36 us
  Pallas kernels: 0 us -> 180 us
  local copies, waits for them, and re-layouts: 127 us -> 9.71 us
  matrix products: 91.4 us -> 0 us
  blocking collectives: 0 us -> 24.3 us
  starting transfers between devices: 8.84 us -> 19.9 us
    another operation x35 -> x0, other arithmetic: 269 us -> none  [the longest x30 173 us: body(): factor = jnp.linalg.cholesky(0.5 * (corner + corner.T))]
    all_to_all x1, waiting for transfers between devices: 216 us -> 0.01 us  [body(): recv1 = lax.all_to_all(rest, 'row', 0, 0)]
    pallas_call x0 -> x3, Pallas kernels: none -> 180 us  [the longest x1 143 us: cholesky(): pl.pallas_call(functools.partial(chol_kernel, n), out_shape=(jax.ShapeDty...]
    psum x1 -> x0, waiting for transfers between devices: 103 us -> none  [from_root(): return lax.psum(jnp.where(mine, value, jnp.zeros_like(value)), axis)]
    dot_general x3 -> x0, matrix products: 47.6 us -> none  [the longest x1 16.7 us: widen_columns(): jnp.einsum('lpxsy,lsb->lpxby', local_rows, chosen, precision=HIGHEST_PREC...]
    another operation x29 -> x0, matrix products: 43.9 us -> none  [the longest x14 23 us: body(): factor = jnp.linalg.cholesky(0.5 * (corner + corner.T))]
    all_gather x2 -> x3, waiting for transfers between devices: 107 us -> 68.5 us  [the longest x1 63.2 us: body(): corner = lax.all_gather(piece, ('row', 'col'))]
    another operation x37 -> x0, local copies, waits for them, and re-layouts: 31.6 us -> none
  transfers between devices with their start and end apart: 4 -> 6, of which waited for: 4 -> 4; matrix products, arithmetic and copies ran while one was open for 2% -> 2% of each run, Pallas kernels for 0% -> 43%
where the time goes in v1:
time: 336 us; the launch traced here: 330 us
  Pallas kernels  180 us (54%)
  waiting for transfers between devices  81.2 us (24%)
  blocking collectives  24.3 us (7%)
  starting transfers between devices  19.9 us (6%)
  between operations  13.2 us (4%)
  local copies, waits for them, and re-layouts  9.71 us (3%)
    pallas_call x1, Pallas kernels, cholesky(): pl.pallas_call(functools.partial(chol_kernel, n), out_shape=(jax.ShapeDty...  143 us
    all_gather x1, waiting for transfers between devices, body(): corner = lax.all_gather(piece, ('row', 'col'))  63.2 us
    pallas_call x1, Pallas kernels, update(): pl.pallas_call(update_kernel, grid=(6,), out_shape=jax.ShapeDtypeStruct((...  34.6 us
    all_to_all x1, blocking collectives, body(): recv0 = lax.all_to_all(slots[:, :, :BS], 'row', 0, 0)  24.3 us
    all_to_all x1, starting transfers between devices, body(): recv1 = lax.all_to_all(rest, 'row', 0, 0)  15.1 us
    ppermute x1, waiting for transfers between devices, body(): lax.ppermute(flat, ('row', 'col'), [(r * 8 + c, (r // 8 * 8 + c) * 8 + r...  11.7 us
    slice x1, local copies, waits for them, and re-layouts, body(): slots[:, :, BS:]  6.85 us
  transfers between devices with their start and end apart: 6, of which 4 were waited for; matrix products, arithmetic and copies ran while one was open for 2% of the time, Pallas kernels for 43%

profile of v1, /device:TPU:1, one launch (start us, length us, event | category | flops | bytes accessed | tf_op | source)
XLA Modules:
  0.0 330.0 jit_solution(10223720181651929917)
XLA Ops:
  6.5 0.0 all-gather.8.cloned.1.call-start
  6.5 1.3 slice.16
  7.9 24.3 %all_to_all.10.recv_ref.recv0_ref = f32[16,128,128]{2,1,0:T(8,128)} all-to-all(f32[16,128,128]{2,1,0:T(8,128)S(1)} %slice.16), channel_id=1, replica_groups=mesh['row'=16,'col'=8] {'row'}, dimensions={0} | all-to-all | bytes 2097152 | tf_op jit(solution)/shard_map/all_to_all | solution.py:281
  32.1 2.3 assemble_panel.1
  34.5 0.8 slice_bitcast_fusion
  35.2 2.8 collective-permute-start
  38.0 1.0 collective-permute-done
  39.0 1.4 fusion
  40.4 0.0 all-gather.8.cloned.1.call-update
  40.4 0.0 copy-start
  40.4 0.0 all-gather.6.cloned.1.call-start
  40.5 6.8 %slice.19 = f32[16,128,896]{2,1,0:T(8,128)} slice(f32[16,128,1024]{2,1,0:T(8,128)} %bitcast.14), slice={[0:16], [0:128], [128:1024]} | slice | bytes 14680064 | tf_op jit(solution)/shard_map/slice | solution.py:286
  47.3 63.2 %all-gather.8.cloned.1.call-done = f32[8192,128]{1,0:T(8,128)} async-done(((f32[64,128]{1,0:T(8,128)}), f32[8192,128]{1,0:T(8,128)}) %all-gather.8.cloned.1.call-update) | async-done | bytes 4194320 | tf_op jit(solution)/shard_map/all_gather | solution.py:285
  110.5 0.0 all-gather.6.cloned.1.call-update
  110.5 0.0 all-gather.10.cloned.1.call-start
  110.6 0.0 copy-done
  110.6 1.9 collective-permute-start.1
  112.5 11.7 %collective-permute-done.1 = f32[768,128]{1,0:T(8,128)S(1)} collective-permute-done((f32[768,128]{1,0:T(8,128)S(1)}, f32[768,128]{1,0:T(8,128)S(1)}, u32[]{:S(2)}, u32[]{:S(2)}) %collective-permute-start.1) | collective-permute-done | bytes 393248 | tf_op jit(solution)/shard_map/ppermute | solution.py:288
  124.2 0.0 copy-start.1
  124.2 0.8 copy-done.1
  124.9 0.0 all-gather.10.cloned.1.call-update
  125.0 15.1 %all-to-all-start.1 = ((f32[16,128,896]{2,1,0:T(8,128)}), f32[16,128,896]{2,1,0:T(8,128)}, u32[]{:S(2)}, u32[]{:S(2)}) async-start(f32[16,128,896]{2,1,0:T(8,128)} %slice.19), calls=%async_computation.1 | async-start | bytes 14680064 | tf_op jit(solution)/shard_map/all_to_all | solution.py:299
  140.0 143.5 %cholesky.1 = (f32[1024,1024]{1,0:T(8,128)}, f32[4,256,256]{2,1,0:T(8,128)}) custom-call(f32[128,64,128]{2,1,0:T(8,128)} %bitcast.20), custom_call_target="tpu_custom_call" | custom-call | flops 99999997952 | bytes 9000000 | tf_op jit(solution)/shard_map/cholesky/pallas_call | solution.py:110
  283.5 0.0 all-gather.6.cloned.1.call-done.rrow_ref
  283.5 0.0 all-to-all-done.1.recv1_ref
  283.5 5.3 %all-gather.10.cloned.1.call-done = f32[12288,128]{1,0:T(8,128)} async-done(((f32[768,128]{1,0:T(8,128)}), f32[12288,128]{1,0:T(8,128)}) %all-gather.10.cloned.1.call-update) | async-done | bytes 6291472 | tf_op jit(solution)/shard_map/all_gather | solution.py:297
  288.8 34.6 %update.1 = f32[6,12,128,128]{3,2,1,0:T(8,128)} custom-call(s32[4,64]{1,0:T(4,128)} %bm_ref.3, s32[4]{0:T(128)} %at_ref.3, f32[6,12,128,128]{3,2,1,0:T(8,128)} %bitcast.16, f32[16,128,128]{2,1,0:T(8,128)} %all_to_all.10.recv_ref.recv0_ref, f32[16,128,896]{2,1,0:T(8,128)} %all-to-all-done.1.recv1_ref, f32[8,768,128]{2,1,0:T(8,128)} %all-gather.6.cloned.1.call-done.rrow_ref, ...), custom_call_target="tpu_custom_call" | custom-call | flops 17999998976 | bytes 36000000 | tf_op jit(solution)/shard_map/update/pallas_call | solution.py:242
Async XLA Ops:
  6.5 104.0 %all-gather.8.cloned.1.call-start = ((), (), s32[]{:S(2)}) async-start(), calls=%async_computation.3 | async-start | bytes 4227072 | tf_op jit(solution)/shard_map/all_gather | solution.py:285
  35.2 3.8 %collective-permute-start = (f32[64,128]{1,0:T(8,128)S(1)}, f32[64,128]{1,0:T(8,128)S(1)}, u32[]{:S(2)}, u32[]{:S(2)}) collective-permute-start(f32[64,128]{1,0:T(8,128)S(1)} %slice_bitcast_fusion), channel_id=1, source_target_pairs={{0,64},{8,72},{16,80},{24,88},{32,96},{40,104},{48,112},{56,120},{... | collective-permute-start | bytes 98312 | tf_op jit(solution)/shard_map/ppermute | solution.py:283
  40.4 70.2 %copy-start = (f32[6,128,128]{2,1,0:T(8,128)S(1)}, f32[6,128,128]{2,1,0:T(8,128)}, u32[]{:S(2)}) copy-start(f32[6,128,128]{2,1,0:T(8,128)} %assemble_panel.1) | copy-start | bytes 1179652
  40.4 243.1 %all-gather.6.cloned.1.call-start = ((), (), s32[]{:S(2)}) async-start(), calls=%async_computation.2 | async-start | bytes 3538944 | tf_op jit(solution)/shard_map/all_gather | solution.py:298
  110.5 178.3 %all-gather.10.cloned.1.call-start = ((), (), s32[]{:S(2)}) async-start(), calls=%async_computation.4 | async-start | bytes 6684672 | tf_op jit(solution)/shard_map/all_gather | solution.py:297
  110.6 13.6 %collective-permute-start.1 = (f32[768,128]{1,0:T(8,128)S(1)}, f32[768,128]{1,0:T(8,128)S(1)}, u32[]{:S(2)}, u32[]{:S(2)}) collective-permute-start(f32[768,128]{1,0:T(8,128)S(1)} %bitcast.18), channel_id=1, source_target_pairs={{0,0},{1,8},{2,16},{3,24},{4,32},{5,40},{6,48},{7,56},{8,1},{9,9},... | collective-permute-start | bytes 1179656 | tf_op jit(solution)/shard_map/ppermute | solution.py:288
  124.2 0.8 copy-start.1
  125.0 158.5 %all-to-all-start.1 = ((f32[16,128,896]{2,1,0:T(8,128)}), f32[16,128,896]{2,1,0:T(8,128)}, u32[]{:S(2)}, u32[]{:S(2)}) async-start(f32[16,128,896]{2,1,0:T(8,128)} %slice.19), calls=%async_computation.1 | async-start | bytes 14680064 | tf_op jit(solution)/shard_map/all_to_all | solution.py:299
Sparse Core Ops, SparseCore 0:
  40.5 69.9 all-gather.7
  112.2 35.3 all-gather.5
  149.8 139.0 all-gather.9

commit v2 on v1

--- a/solution.py
+++ b/solution.py
@@ -64,12 +64,12 @@
     lax.fori_loop(0, 16, panel, (tuple(d), tuple(x)))
 
 
-def chol_kernel(n, c_ref, l_ref, m_ref, u_ref, x_ref):
+def chol_kernel(n, c_ref, l_ref, m_ref, u_ref, x_ref, hook):
     def blk(i, j):
         return (pl.ds(i * BS, BS), pl.ds(j * BS, BS))
 
     def corner(i, j):
-        return jnp.concatenate([c_ref[i * n + j], c_ref[(i + n) * n + j]], axis=0)
+        return jnp.concatenate([c_ref[i, j], c_ref[i + n, j]], axis=0)
 
     for i in range(n):
         for j in range(i + 1):
@@ -93,6 +93,8 @@
             m_ref[k // 2, 0:BS, BS : 2 * BS] = jnp.zeros((BS, BS), F32)
             t = mm(l_ref[blk(k, k - 1)], m_ref[k // 2, 0:BS, 0:BS], NN)
             m_ref[k // 2, BS : 2 * BS, 0:BS] = -mm(x, t, NN)
+        if k == 2:
+            hook()
         if k + 1 < n:
             lo = (k + 1) * BS
             rest = n * BS - lo
@@ -105,53 +107,210 @@
                 )
 
 
-def cholesky(corner):
-    n = 8
-    return pl.pallas_call(
-        functools.partial(chol_kernel, n),
-        out_shape=(
-            jax.ShapeDtypeStruct((n * BS, n * BS), F32),
-            jax.ShapeDtypeStruct((n // 2, 2 * BS, 2 * BS), F32),
-        ),
-        in_specs=[VMEM_SPEC],
-        out_specs=(VMEM_SPEC, VMEM_SPEC),
-        scratch_shapes=[pltpu.VMEM((BS, BS), F32), pltpu.VMEM((BS, BS), F32)],
-        cost_estimate=pl.CostEstimate(
-            flops=100_000_000_000, bytes_accessed=9_000_000, transcendentals=0
-        ),
-        name="cholesky",
-    )(corner)
-
-
-def assemble_kernel(bm_ref, at_ref, front_ref, recv_ref, out_ref):
+ORDER = (
+    (2, 2), (1, 1), (3, 3), (0, 2), (2, 0), (1, 3), (3, 1), (2, 1),
+    (1, 2), (3, 2), (2, 3), (0, 1), (1, 0), (0, 3), (3, 0),
+)
+MESH = pl.DeviceIdType.MESH
+
+
+def exchange_kernel(
+    bm_ref, at_ref, front_ref, child_ref,
+    recv0_ref, recv1_ref, rrow_ref, rcol_ref, l_ref, m_ref,
+    small, panel, fr, c1, cbuf, seg, own, u_ref, x_ref, loc, snd, rcv,
+):
     p = lax.axis_index("row")
     q = lax.axis_index("col")
-    out_ref[...] = front_ref[:, 0]
+    px, pz = p // 4, p % 4
+    par = q % 2
+    home = p % 8
+
+    def peer(d):
+        return ((px + d[0]) % 4) * 4 + (pz + d[1]) % 4
+
+    def send(src, dst, i, to):
+        pltpu.make_async_remote_copy(
+            src_ref=src, dst_ref=dst, send_sem=snd.at[i], recv_sem=rcv.at[i],
+            device_id=to, device_id_type=MESH,
+        ).start()
+
+    def local(src, dst, sem):
+        return pltpu.make_async_copy(src, dst, sem)
+
+    def wait(ref, sem):
+        pltpu.make_async_copy(ref, ref, sem).wait()
+
+    barrier = pltpu.get_barrier_semaphore()
+
+    def hello(to):
+        pl.semaphore_signal(barrier, inc=1, device_id=to, device_id_type=MESH)
+
+    for d in ORDER:
+        hello((peer(d), q))
+    for i in range(1, 8):
+        hello((p, (q + i) % 8))
+    slot = (p // 8) * 8 + q
+
+    @pl.when(home != q)
+    def _():
+        hello((slot, home))
+
+    @pl.when(p >= 8)
+    def _():
+        for i in range(8):
+            hello((p - 8, i))
+
+    pl.semaphore_wait(barrier, 23 - jnp.where(home == q, 1, 0) + jnp.where(p < 8, 8, 0))
+
+    for d in ORDER:
+        send(child_ref.at[peer(d), :, pl.ds(0, BS)], small.at[p], 0, (peer(d), q))
+    local(child_ref.at[p, :, pl.ds(0, BS)], small.at[p], rcv.at[0]).start()
+    front_copy = local(front_ref.at[:, 0], fr, loc.at[0])
+    front_copy.start()
+    own_copy = local(child_ref.at[p, :, pl.ds(BS, 7 * BS)], own, loc.at[1])
+    own_copy.start()
+    front_copy.wait()
+    wait(small, rcv.at[0])
+    weights = []
     for c in range(CHILD):
         k = at_ref[c]
         hit = bm_ref[k, q] == q
         for t in range(4):
             r = bm_ref[k, t * 16 + p]
-
-            @pl.when(jnp.logical_and(hit, r >= 0))
-            def _(r=r, s=c * 4 + t):
-                out_ref[r >> 4] += recv_ref[s]
-
-
-def assemble_panel(block_map, child_at, front, recv):
+            weights.append(
+                [jnp.where(jnp.logical_and(hit, r == a * 16 + p), 1.0, 0.0) for a in range(6)]
+            )
+    for a in range(6):
+        acc = fr[a]
+        for s in range(16):
+            acc = acc + weights[s][a] * small[s]
+        panel[a] = acc
+
+    @pl.when(p < 8)
+    def _():
+        top, low = panel.at[0, pl.ds(0, 64)], panel.at[0, pl.ds(64, 64)]
+        for i in range(1, 8):
+            send(top, c1.at[q], 1, (p, (q + i) % 8))
+        local(top, c1.at[q], rcv.at[1]).start()
+        for i in range(8):
+            send(low, c1.at[q], 1, (p + 8, (q + i) % 8))
+
+    @pl.when(home == q)
+    def _():
+        local(panel, seg, rcv.at[4]).start()
+
+    @pl.when(home != q)
+    def _():
+        send(panel, seg, 4, (slot, home))
+
+    wait(c1, rcv.at[1])
+
+    for b in range(2):
+        half = pl.ds(par * 4 + 2 * b, 2)
+        for d in ORDER:
+            send(c1.at[half], cbuf.at[p, half], 3, (peer(d), q))
+        local(c1.at[half], cbuf.at[p, half], rcv.at[3]).start()
+
+    def send_rows(a, carry):
+        rows = pl.ds(pl.multiple_of(a * BS, BS), BS)
+        for i in range(1, 8):
+            send(panel.at[a], rrow_ref.at[q, rows], 2, (p, (q + i) % 8))
+        local(panel.at[a], rrow_ref.at[q, rows], rcv.at[2]).start()
+        return carry
+
+    mine = cbuf.at[:, pl.ds(par * 4, 4)]
+    wait(mine, rcv.at[3])
+    send(mine, mine, 5, (p, q + 1 - 2 * par))
+    lax.fori_loop(0, 6, send_rows, 0)
+
+    upper, lower = pl.ds(0, 3), pl.ds(3, 3)
+    wait(seg, rcv.at[4])
+    for i in range(1, 4):
+        send(seg.at[upper], rcol_ref.at[px, pz, upper], 7, (peer((0, i)), q))
+        send(seg.at[lower], rcol_ref.at[px, pz, lower], 7, (peer((i, 0)), q))
+    seg_copy = local(seg, rcol_ref.at[px, pz], loc.at[0])
+    seg_copy.start()
+
+    def forward():
+        wait(rcol_ref.at[0, pl.ds(0, 3)], rcv.at[7])
+        seg_copy.wait()
+        for j in range(4):
+            for i in range(1, 4):
+                piece = rcol_ref.at[px, j, upper]
+                send(piece, piece, 8, (peer((i, 0)), q))
+                piece = rcol_ref.at[j, pz, lower]
+                send(piece, piece, 8, (peer((0, i)), q))
+
+    def send_slots(c, carry):
+        rows = pl.ds(pl.multiple_of(c * 16, 16), 16)
+        cols = pl.ds(BS, 7 * BS)
+        for d in ORDER:
+            send(child_ref.at[peer(d), rows, cols], recv1_ref.at[p, rows], 6, (peer(d), q))
+        return carry
+
+    lax.fori_loop(0, 8, send_slots, 0)
+    own_copy.wait()
+    local(own, recv1_ref.at[p], rcv.at[6]).start()
+    recv0_copy = local(small, recv0_ref, loc.at[1])
+    recv0_copy.start()
+    wait(cbuf.at[:, pl.ds(4 - par * 4, 4)], rcv.at[5])
+    chol_kernel(8, cbuf, l_ref, m_ref, u_ref, x_ref, forward)
+    recv0_copy.wait()
+    wait(rrow_ref, rcv.at[2])
+    wait(rcol_ref.at[pl.ds(0, 3)], rcv.at[8])
+    wait(recv1_ref, rcv.at[6])
+    wait(small.at[pl.ds(0, 15)], snd.at[0])
+    wait(rrow_ref.at[pl.ds(0, 7)], snd.at[2])
+    wait(cbuf.at[pl.ds(0, 15), pl.ds(0, 4)], snd.at[3])
+    wait(rcol_ref.at[0, pl.ds(0, 3)], snd.at[7])
+    wait(rcol_ref.at[pl.ds(0, 3)], snd.at[8])
+
+    @pl.when(p < 8)
+    def _():
+        wait(c1, snd.at[1])
+        wait(c1.at[pl.ds(0, 7)], snd.at[1])
+
+    @pl.when(home != q)
+    def _():
+        wait(seg, snd.at[4])
+
+    wait(mine, snd.at[5])
+    wait(recv1_ref.at[pl.ds(0, 15)], snd.at[6])
+
+
+def exchange(block_map, child_at, front, children):
+    any_spec = pl.BlockSpec(memory_space=pl.ANY)
     return pl.pallas_call(
-        assemble_kernel,
-        grid=(1,),
-        out_shape=jax.ShapeDtypeStruct((6, BS, BS), F32),
-        in_specs=[
-            SMEM_SPEC,
-            SMEM_SPEC,
-            pl.BlockSpec((6, 1, BS, BS), lambda i: (0, 0, 0, 0)),
-            pl.BlockSpec((16, BS, BS), lambda i: (0, 0, 0)),
+        exchange_kernel,
+        out_shape=(
+            jax.ShapeDtypeStruct((16, BS, BS), F32),
+            jax.ShapeDtypeStruct((16, BS, 7 * BS), F32),
+            jax.ShapeDtypeStruct((8, 6 * BS, BS), F32),
+            jax.ShapeDtypeStruct((4, 4, 6, BS, BS), F32),
+            jax.ShapeDtypeStruct((8 * BS, 8 * BS), F32),
+            jax.ShapeDtypeStruct((4, 2 * BS, 2 * BS), F32),
+        ),
+        in_specs=[SMEM_SPEC, SMEM_SPEC, any_spec, any_spec],
+        out_specs=(any_spec, any_spec, any_spec, any_spec, VMEM_SPEC, VMEM_SPEC),
+        scratch_shapes=[
+            pltpu.VMEM((16, BS, BS), F32),
+            pltpu.VMEM((6, BS, BS), F32),
+            pltpu.VMEM((6, BS, BS), F32),
+            pltpu.VMEM((8, 64, BS), F32),
+            pltpu.VMEM((16, 8, 64, BS), F32),
+            pltpu.VMEM((6, BS, BS), F32),
+            pltpu.VMEM((BS, 7 * BS), F32),
+            pltpu.VMEM((BS, BS), F32),
+            pltpu.VMEM((BS, BS), F32),
+            pltpu.SemaphoreType.DMA((2,)),
+            pltpu.SemaphoreType.DMA((9,)),
+            pltpu.SemaphoreType.DMA((9,)),
         ],
-        out_specs=pl.BlockSpec((6, BS, BS), lambda i: (0, 0, 0)),
-        name="assemble_panel",
-    )(block_map, child_at, front, recv)
+        compiler_params=pltpu.CompilerParams(
+            collective_id=1, has_side_effects=True, vmem_limit_bytes=60 * 1024 * 1024
+        ),
+        name="exchange",
+    )(block_map, child_at, front, children)
 
 
 def update_kernel(
@@ -275,30 +434,11 @@
 
 
 def body(front, children, block_map, child_at):
-    p = lax.axis_index("row")
     front4 = front.transpose(0, 2, 1, 3)
-    slots = children.reshape(16, BS, 8 * BS)
-    recv0 = lax.all_to_all(slots[:, :, :BS], "row", 0, 0)
-    panel = assemble_panel(block_map, child_at, front4, recv0)
-    low = lax.ppermute(panel[0, 64:], "row", [(i, i + 8) for i in range(8)])
-    piece = jnp.where(p < 8, panel[0, :64], low)
-    corner = lax.all_gather(piece, ("row", "col"))
-    corner, panel, rest = lax.optimization_barrier((corner, panel, slots[:, :, BS:]))
-    flat = panel.reshape(768, BS)
-    moved = lax.ppermute(
-        flat,
-        ("row", "col"),
-        [
-            (r * 8 + c, ((r // 8) * 8 + c) * 8 + r % 8)
-            for r in range(16)
-            for c in range(8)
-        ],
+    recv0, recv1, rrow, rcol, l, m = exchange(
+        block_map, child_at, front4, children.reshape(16, BS, 8 * BS)
     )
-    rcol = lax.all_gather(moved, "row")
-    rrow = lax.all_gather(flat, "col")
-    recv1 = lax.all_to_all(rest, "row", 0, 0)
-    l, m = cholesky(corner)
-    out = update(block_map, child_at, front4, recv0, recv1, rrow, rcol, l, m)
+    out = update(block_map, child_at, front4, recv0, recv1, rrow, rcol.reshape(16, 6 * BS, BS), l, m)
     return out.transpose(0, 2, 1, 3)
 
 

time: 336 us -> 249 us (0.74); the launches traced: 330 us -> 249 us
  waiting for transfers between devices: 81.2 us -> 0 us
  Pallas kernels: 180 us -> 249 us
  blocking collectives: 24.3 us -> 0 us
  starting transfers between devices: 19.9 us -> 0 us
  between operations: 13.2 us -> 0.01 us
  local copies, waits for them, and re-layouts: 9.71 us -> 0 us
    all_gather x3 -> x0, waiting for transfers between devices: 68.5 us -> none  [the longest x1 63.2 us: body(): corner = lax.all_gather(piece, ('row', 'col'))]
    pallas_call x2 -> x1, Pallas kernels: 146 us -> 214 us  [exchange(): pl.pallas_call(exchange_kernel, out_shape=(jax.ShapeDtypeStruct((16, BS,...]
    all_to_all x1 -> x0, blocking collectives: 24.3 us -> none  [body(): recv0 = lax.all_to_all(slots[:, :, :BS], 'row', 0, 0)]
    all_to_all x1 -> x0, starting transfers between devices: 15.1 us -> none  [body(): recv1 = lax.all_to_all(rest, 'row', 0, 0)]
    ppermute x2 -> x0, waiting for transfers between devices: 12.7 us -> none  [the longest x1 11.7 us: body(): lax.ppermute(flat, ('row', 'col'), [(r * 8 + c, (r // 8 * 8 + c) * 8 + r...]
    slice x2 -> x0, local copies, waits for them, and re-layouts: 8.17 us -> none  [the longest x1 6.85 us: body(): slots[:, :, BS:]]
    ppermute x2 -> x0, starting transfers between devices: 4.72 us -> none  [the longest x1 2.8 us: body(): low = lax.ppermute(panel[0, 64:], 'row', [(i, i + 8) for i in range(8)])]
  transfers between devices with their start and end apart: 6 -> 0, of which waited for: 4 -> 0; matrix products, arithmetic and copies ran while one was open for 2% -> 0% of each run, Pallas kernels for 43% -> 0%
where the time goes in v2:
time: 249 us
  Pallas kernels  249 us (100%)
    pallas_call x1, Pallas kernels, exchange(): pl.pallas_call(exchange_kernel, out_shape=(jax.ShapeDtypeStruct((16, BS,...  214 us
    pallas_call x1, Pallas kernels, update(): pl.pallas_call(update_kernel, grid=(6,), out_shape=jax.ShapeDtypeStruct((...  35.1 us

profile of v2, /device:TPU:1, one launch (start us, length us, event | category | flops | bytes accessed | tf_op | source)
XLA Modules:
  0.0 248.8 jit_solution(5592212466639138572)
XLA Ops:
  0.0 213.6 %exchange.1 = (f32[16,128,128]{2,1,0:T(8,128)}, f32[16,128,896]{2,1,0:T(8,128)}, f32[8,768,128]{2,1,0:T(8,128)}, f32[4,4,6,128,128]{4,3,2,1,0:T(8,128)}, f32[1024,1024]{1,0:T(8,128)}, /*index=5*/f32[4,256,256]{2,1,0:T(8,128)}) custom-call(s32[4,64]{1,0:T(4,128)} %bm_ref.3, s32[4]{0:T(128)} %at_ref.3, f32[6,12,128,128]{3,2,1,0:T(8,128)} %bitcast.5, ...), custom_call_target="tpu_custom_call" | custom-call | tf_op jit(solution)/shard_map/exchange/pallas_call | solution.py:283
  213.6 35.1 %update.1 = f32[6,12,128,128]{3,2,1,0:T(8,128)} custom-call(s32[4,64]{1,0:T(4,128)} %bm_ref.3, s32[4]{0:T(128)} %at_ref.3, f32[6,12,128,128]{3,2,1,0:T(8,128)} %bitcast.6, f32[16,128,128]{2,1,0:T(8,128)} %get-tuple-element.11.recv0_ref, f32[16,128,896]{2,1,0:T(8,128)} %get-tuple-element.12.recv1_ref, f32[8,768,128]{2,1,0:T(8,128)} %get-tuple-element.13.rrow_ref, ...), custom_call_target="tpu_custom_call" | custom-call | flops 17999998976 | bytes 36000000 | tf_op jit(solution)/shard_map/update/pallas_call | solution.py:401
